TPU v7x, 32 devices: a whole 2x2x4 slice. The times are simulated.
32 devices in a mesh: harm: 4 (over y, x), slab: 8 (over z, core).
Axes of the slice: x: 2, y: 2, z: 4, core: 2. Of those that a mesh axis runs over, the one named last changes fastest.
Arguments:
- krylov_basis: float32 [3, 4, 4, 16, 32, 128], P(None, 'harm', None, 'slab'), may hold values from -16 to 16
- weights: float32 [3], replicated, may hold values from -3 to 3
- base_flow: bfloat16 [4, 3, 16, 32, 128], P('harm', None, 'slab'), may hold values from -4 to 4
- shifts: float32 [4], P('harm'), may hold values from 0.25 to 2
Outputs:
- next_vector: float32 [4, 4, 16, 32, 128], P('harm', None, 'slab')
- arnoldi_column: float32 [4], replicated
All inputs are finite; a program needn't handle non-finite values.
Results may differ from a plain program's by a relative error of at most 0.009.
Values may be sent and summed in bfloat16 or wider, within the bound.
No kernel may reach another device: no remote copies, remote signals or barrier semaphores. Data moves between devices by JAX's collectives and lax.ppermute only.
A program may use at most 64 MiB of HBM per device.

v0:
```python
import jax
import jax.numpy as jnp
from jax import lax
from jax.sharding import PartitionSpec as P

SWEEPS = 4
viscosity = 1.0
epsilon = 1e-06


def padded_2(cells, sides, width):
    for axis, dim in sides:
        count = lax.axis_size(axis)
        ends = count - 1
        head = lax.slice_in_dim(cells, 0, width, axis=dim)
        tail = lax.slice_in_dim(cells, cells.shape[dim] - width, cells.shape[dim], axis=dim)
        cells = jnp.concatenate(
            [
                lax.ppermute(tail, axis, [(i, (i + 1) % count) for i in range(ends)]),
                cells,
                lax.ppermute(head, axis, [((i + 1) % count, i) for i in range(ends)]),
            ],
            axis=dim,
        )
    return cells


def broadcast(x, axis, root):
    mine = lax.axis_index(axis) == root
    return lax.psum(jnp.where(mine, x, jnp.zeros_like(x)), axis)


def shifted(value, axis, steps):
    count = lax.axis_size(axis)
    pairs = [(source, (source + steps) % count) for source in range(count)]
    return lax.ppermute(value, axis, pairs)


def neighbours_y(values):
    padded = jnp.pad(values, ((0, 0), (0, 0), (1, 1), (0, 0)))
    return (padded[:, :, 2:], padded[:, :, :-2])


def laplace_ext(extended):
    center = extended[:, 1:-1]
    upper_y, lower_y = neighbours_y(center)
    result = extended[:, 2:] + extended[:, :-2] + upper_y + lower_y
    result = result + jnp.roll(center, -1, axis=3) + jnp.roll(center, 1, axis=3)
    return result - 6.0 * center


def divergence_split(flux_x, flux_y, flux_z):
    upper_y, lower_y = neighbours_y(flux_y)
    result = 0.5 * (flux_x[:, 2:] - flux_x[:, :-2])
    result = result + 0.5 * (upper_y - lower_y)
    return result + 0.5 * (jnp.roll(flux_z, -1, axis=3) - jnp.roll(flux_z, 1, axis=3))


def sweep_extend(values):
    return padded_2(values, (("slab", 1),), 1)


def chebyshev(applied, shift_value):
    middle = shift_value + 6.0 * viscosity
    half_span = 6.0 * viscosity
    span_ratio = middle / half_span
    solution = jnp.zeros_like(applied)
    remainder = applied
    direction = applied / middle
    ratio_prev = 1.0 / span_ratio
    for sweep_index in range(SWEEPS):
        solution = solution + direction
        remainder = remainder - (
            shift_value * direction - viscosity * laplace_ext(sweep_extend(direction))
        )
        ratio_next = 1.0 / (2.0 * span_ratio - ratio_prev)
        direction = ratio_next * ratio_prev * direction + 2.0 * ratio_next / half_span * remainder
        ratio_prev = ratio_next
    return solution + direction


def shards(krylov_basis, weights, base_flow, shifts):
    vectors = krylov_basis[:, 0]
    start_vec = jnp.sum(weights[:, None, None, None, None] * vectors, axis=0)
    harm_count = lax.axis_size("harm") * base_flow.shape[0]
    local_flow = base_flow[0]
    cell_shape = start_vec.shape
    empty = jnp.zeros((3,) + cell_shape, jnp.float32)

    def add_term(fluxes, current, cycle_step):
        shared = broadcast(local_flow, "harm", cycle_step).astype(jnp.float32)
        return fluxes + shared[:, None] * current[None]

    def advance(cycle_step, carried):
        fluxes, current = carried
        fluxes = add_term(fluxes, current, cycle_step)
        return (fluxes, shifted(current, "harm", 1))

    fluxes, current = lax.fori_loop(0, harm_count - 1, advance, (empty, start_vec))
    fluxes = add_term(fluxes, current, harm_count - 1)
    fluxes = fluxes.reshape((12,) + cell_shape[1:])
    stacked = jnp.concatenate([fluxes, start_vec], axis=0)
    extended = padded_2(stacked, (("slab", 1),), 1)
    moved = divergence_split(extended[0:4], extended[4:8, 1:-1], extended[8:12, 1:-1])
    field_ext = extended[12:]
    own_shift = shifts[0]
    applied = own_shift * start_vec - viscosity * laplace_ext(field_ext) + moved
    solution = chebyshev(applied, own_shift)
    entries = float(
        harm_count
        * cell_shape[0]
        * cell_shape[1]
        * lax.axis_size("slab")
        * cell_shape[2]
        * cell_shape[3]
    )
    local_proj = jnp.sum(vectors * solution[None], axis=(1, 2, 3, 4))
    projection = lax.psum(local_proj, ("harm", "slab")) / entries
    residue = solution - jnp.sum(projection[:, None, None, None, None] * vectors, axis=0)
    square = lax.psum(jnp.sum(residue * residue), ("harm", "slab")) / entries
    norm_value = jnp.sqrt(square + epsilon)
    next_vector = (residue / norm_value)[None]
    arnoldi_column = jnp.concatenate([projection, norm_value[None]])
    return (next_vector, arnoldi_column)


def solution(mesh):
    in_specs = (
        P(None, "harm", None, "slab", None, None),
        P(),
        P("harm", None, "slab", None, None),
        P("harm"),
    )
    out_specs = (P("harm", None, "slab", None, None), P())
    return jax.shard_map(shards, mesh=mesh, in_specs=in_specs, out_specs=out_specs, check_vma=False)
```

profile of v0, /device:TPU:0, one launch (start us, length us, event | category | flops | bytes accessed | tf_op | source)
XLA Modules:
  0.0 199.5 jit_solution(12436300417976476142)
XLA Ops:
  0.6 0.0 copy-start.5
  0.7 0.6 copy-done.5
  1.3 1.1 fusion
  2.4 0.0 copy-start
  2.4 0.0 copy-start.4
  2.4 0.6 copy-done
  3.1 0.2 copy-done.4
  3.3 18.4 %psum.32 = bf16[3,2,32,128]{3,2,1,0:T(8,128)(2,1)S(1)} all-reduce(bf16[3,2,32,128]{3,2,1,0:T(8,128)(2,1)S(1)} %broadcast_select_fusion.1), channel_id=1, replica_groups=mesh['harm'=4,'slab'=8] {'harm'}, use_global_device_ids=true, to_apply=%region_4.5 | all-reduce | flops 24576 | bytes 98304 | tf_op jit(solution)/shard_map/psum | solution.py:30
  21.7 52.6 %while.16 = (s32[]{:T(128)}, f32[3,4,2,32,128]{4,3,2,1,0:T(8,128)S(1)}, f32[4,2,32,128]{3,2,1,0:T(8,128)S(1)}, bf16[3,2,32,128]{3,2,1,0:T(8,128)(2,1)S(1)}, s32[]{:T(128)}, /*index=5*/u32[]{:T(128)}, s32[]{:T(128)}) while((s32[]{:T(128)}, f32[3,4,2,32,128]{4,3,2,1,0:T(8,128)S(1)}, f32[4,2,32,128]{3,2,1,0:T(8,128)S(1)}, ...), condition=%wide.region_3.4_spmd.clone, body=%wide.region_1.3_spmd.clone.sunk | while | flops 368647 | bytes 2146473 | solution.py:99
  21.7 0.1 collective-permute-start
  21.8 17.2 %psum.37 = bf16[3,2,32,128]{3,2,1,0:T(8,128)(2,1)S(1)} all-reduce(bf16[3,2,32,128]{3,2,1,0:T(8,128)(2,1)S(1)} %broadcast_select_fusion.3), channel_id=1, replica_groups=mesh['harm'=4,'slab'=8] {'harm'}, use_global_device_ids=true, to_apply=%region_2.2 | all-reduce | flops 24576 | bytes 98304 | tf_op jit(solution)/shard_map/while/body/eval_jaxpr/psum | solution.py:30
  39.1 0.1 select_add_fusion.2
  39.2 0.0 collective-permute-done
  39.3 0.1 collective-permute-start
  39.4 17.3 %psum.37 = bf16[3,2,32,128]{3,2,1,0:T(8,128)(2,1)S(1)} all-reduce(bf16[3,2,32,128]{3,2,1,0:T(8,128)(2,1)S(1)} %broadcast_select_fusion.3), channel_id=1, replica_groups=mesh['harm'=4,'slab'=8] {'harm'}, use_global_device_ids=true, to_apply=%region_2.2 | all-reduce | flops 24576 | bytes 98304 | tf_op jit(solution)/shard_map/while/body/eval_jaxpr/psum | solution.py:30
  56.7 0.1 select_add_fusion.2
  56.8 0.1 collective-permute-start
  56.9 17.1 %psum.37 = bf16[3,2,32,128]{3,2,1,0:T(8,128)(2,1)S(1)} all-reduce(bf16[3,2,32,128]{3,2,1,0:T(8,128)(2,1)S(1)} %broadcast_select_fusion.3), channel_id=1, replica_groups=mesh['harm'=4,'slab'=8] {'harm'}, use_global_device_ids=true, to_apply=%region_2.2 | all-reduce | flops 24576 | bytes 98304 | tf_op jit(solution)/shard_map/while/body/eval_jaxpr/psum | solution.py:30
  74.1 0.1 select_add_fusion.2
  74.2 0.0 collective-permute-done
  74.3 0.0 copy-start.1
  74.3 0.1 multiply_add_fusion
  74.3 0.8 copy-done.1
  75.2 1.3 collective-permute-start.1
  76.5 3.0 %collective-permute-start.2 = (f32[16,1,32,128]{3,2,1,0:T(8,128)S(1)}, f32[16,1,32,128]{3,2,1,0:T(8,128)S(1)}, u32[]{:S(2)}, u32[]{:S(2)}) collective-permute-start(f32[16,1,32,128]{3,2,1,0:T(8,128)S(1)} %get-tuple-element.118), channel_id=1, source_target_pairs={{0,1},{1,2},{2,3},{3,4},{4,5},{5,6},{6,7},{8,9},{9,10},{10,11},{11... | collective-permute-start | bytes 786440 | tf_op jit(solution)/shard_map/ppermute | solution.py:19
  79.6 0.1 fusion.69
  79.7 0.1 fusion.70
  79.8 0.1 fusion.67
  80.8 0.1 fusion.68
  80.9 0.0 collective-permute-done.1
  80.9 0.0 collective-permute-done.2
  80.9 0.2 broadcast_divide_fusion
  81.1 0.1 fusion.65
  81.2 1.3 collective-permute-start.3
  82.5 5.7 %collective-permute-start.4 = (f32[4,1,32,128]{3,2,1,0:T(8,128)S(1)}, f32[4,1,32,128]{3,2,1,0:T(8,128)S(1)}, u32[]{:S(2)}, u32[]{:S(2)}) collective-permute-start(f32[4,1,32,128]{3,2,1,0:T(8,128)S(1)} %get-tuple-element.140), channel_id=1, source_target_pairs={{0,1},{1,2},{2,3},{3,4},{4,5},{5,6},{6,7},{8,9},{9,10},{10,11},{11... | collective-permute-start | bytes 196616 | tf_op jit(solution)/shard_map/ppermute | solution.py:19
  88.2 0.1 fusion.66
  88.3 0.8 collective-permute-done.4
  89.1 0.1 multiply_add_fusion.3
  89.3 0.1 fusion.62
  89.4 1.3 collective-permute-start.5
  90.7 5.4 %collective-permute-start.6 = (f32[4,1,32,128]{3,2,1,0:T(8,128)S(1)}, f32[4,1,32,128]{3,2,1,0:T(8,128)S(1)}, u32[]{:S(2)}, u32[]{:S(2)}) collective-permute-start(f32[4,1,32,128]{3,2,1,0:T(8,128)S(1)} %get-tuple-element.134), channel_id=1, source_target_pairs={{0,1},{1,2},{2,3},{3,4},{4,5},{5,6},{6,7},{8,9},{9,10},{10,11},{11... | collective-permute-start | bytes 196616 | tf_op jit(solution)/shard_map/ppermute | solution.py:19
  96.1 0.1 fusion.63
  96.2 0.8 collective-permute-done.6
  97.0 0.1 multiply_add_fusion.2
  97.2 0.1 fusion.59
  97.3 1.3 collective-permute-start.7
  98.6 5.3 %collective-permute-start.8 = (f32[4,1,32,128]{3,2,1,0:T(8,128)S(1)}, f32[4,1,32,128]{3,2,1,0:T(8,128)S(1)}, u32[]{:S(2)}, u32[]{:S(2)}) collective-permute-start(f32[4,1,32,128]{3,2,1,0:T(8,128)S(1)} %get-tuple-element.128), channel_id=1, source_target_pairs={{0,1},{1,2},{2,3},{3,4},{4,5},{5,6},{6,7},{8,9},{9,10},{10,11},{11... | collective-permute-start | bytes 196616 | tf_op jit(solution)/shard_map/ppermute | solution.py:19
  103.9 0.1 fusion.60
  104.0 0.8 collective-permute-done.8
  104.8 0.1 multiply_add_fusion.1
  104.9 0.1 fusion.55
  105.1 4.7 %collective-permute-start.10 = (f32[4,1,32,128]{3,2,1,0:T(8,128)S(1)}, f32[4,1,32,128]{3,2,1,0:T(8,128)S(1)}, u32[]{:S(2)}, u32[]{:S(2)}) collective-permute-start(f32[4,1,32,128]{3,2,1,0:T(8,128)S(1)} %get-tuple-element.126), channel_id=1, source_target_pairs={{0,1},{1,2},{2,3},{3,4},{4,5},{5,6},{6,7},{8,9},{9,10},{10,11},{11... | collective-permute-start | bytes 196616 | tf_op jit(solution)/shard_map/ppermute | solution.py:19
  109.8 1.3 collective-permute-start.9
  111.1 0.1 fusion.56
  111.2 3.6 %collective-permute-done.9 = f32[4,1,32,128]{3,2,1,0:T(8,128)S(1)} collective-permute-done((f32[4,1,32,128]{3,2,1,0:T(8,128)S(1)}, f32[4,1,32,128]{3,2,1,0:T(8,128)S(1)}, u32[]{:S(2)}, u32[]{:S(2)}) %collective-permute-start.9) | collective-permute-done | bytes 65568 | tf_op jit(solution)/shard_map/ppermute | solution.py:21
  114.8 0.2 fusion.45
  114.9 0.8 copy-done.3
  115.8 0.1 fusion.1
  115.9 40.9 %psum.33 = f32[3]{0:T(128)S(1)} all-reduce(f32[3]{0:T(128)S(1)} %fusion.1), channel_id=1, replica_groups=mesh['harm'=4,'slab'=8] {'harm','slab'}, use_global_device_ids=true, to_apply=%region_6.7 | all-reduce | flops 3 | bytes 24 | tf_op jit(solution)/shard_map/psum | solution.py:118
  156.9 0.1 fusion.2
  157.0 0.6 multiply_reduce_fusion
  157.6 39.9 %psum.34 = f32[]{:T(128)} all-reduce(f32[]{:T(128)} %get-tuple-element.107), channel_id=1, replica_groups=mesh['harm'=4,'slab'=8] {'harm','slab'}, use_global_device_ids=true, to_apply=%region_9.10 | all-reduce | flops 1 | bytes 8 | tf_op jit(solution)/shard_map/psum | solution.py:120
  198.2 0.6 pad_maximum_fusion.13
  198.8 0.7 divide_bitcast_fusion
  (27 shorter events, 0.2 us)
Async XLA Ops:
  0.6 0.7 copy-start.5
  2.4 0.7 copy-start
  2.4 0.8 copy-start.4
  3.3 18.4 %copy-start.2 = (f32[4,2,32,128]{3,2,1,0:T(8,128)S(1)}, f32[4,2,32,128]{3,2,1,0:T(8,128)}, u32[]{:S(2)}) copy-start(f32[4,2,32,128]{3,2,1,0:T(8,128)} %copy-done) | copy-start | bytes 393220
  21.7 17.5 %collective-permute-start = (f32[4,2,32,128]{3,2,1,0:T(8,128)S(1)}, f32[4,2,32,128]{3,2,1,0:T(8,128)S(1)}, u32[]{:S(2)}, u32[]{:S(2)}) collective-permute-start(f32[4,2,32,128]{3,2,1,0:T(8,128)S(1)} %copy.11), channel_id=1, source_target_pairs={{0,8},{8,16},{16,24},{24,0},{1,9},{9,17},{17,25},{25,1},{2,10},{10... | collective-permute-start | bytes 393224 | tf_op jit(solution)/shard_map/while/body/eval_jaxpr/ppermute | solution.py:36
  39.3 17.5 %collective-permute-start = (f32[4,2,32,128]{3,2,1,0:T(8,128)S(1)}, f32[4,2,32,128]{3,2,1,0:T(8,128)S(1)}, u32[]{:S(2)}, u32[]{:S(2)}) collective-permute-start(f32[4,2,32,128]{3,2,1,0:T(8,128)S(1)} %copy.11), channel_id=1, source_target_pairs={{0,8},{8,16},{16,24},{24,0},{1,9},{9,17},{17,25},{25,1},{2,10},{10... | collective-permute-start | bytes 393224 | tf_op jit(solution)/shard_map/while/body/eval_jaxpr/ppermute | solution.py:36
  56.8 17.4 %collective-permute-start = (f32[4,2,32,128]{3,2,1,0:T(8,128)S(1)}, f32[4,2,32,128]{3,2,1,0:T(8,128)S(1)}, u32[]{:S(2)}, u32[]{:S(2)}) collective-permute-start(f32[4,2,32,128]{3,2,1,0:T(8,128)S(1)} %copy.11), channel_id=1, source_target_pairs={{0,8},{8,16},{16,24},{24,0},{1,9},{9,17},{17,25},{25,1},{2,10},{10... | collective-permute-start | bytes 393224 | tf_op jit(solution)/shard_map/while/body/eval_jaxpr/ppermute | solution.py:36
  74.3 0.9 copy-start.1
  75.2 5.7 %collective-permute-start.1 = (f32[16,1,32,128]{3,2,1,0:T(8,128)S(1)}, f32[16,1,32,128]{3,2,1,0:T(8,128)S(1)}, u32[]{:S(2)}, u32[]{:S(2)}) collective-permute-start(f32[16,1,32,128]{3,2,1,0:T(8,128)S(1)} %get-tuple-element.117), channel_id=1, source_target_pairs={{1,0},{2,1},{3,2},{4,3},{5,4},{6,5},{7,6},{9,8},{10,9},{11,10},{12... | collective-permute-start | bytes 786440 | tf_op jit(solution)/shard_map/ppermute | solution.py:21
  76.5 4.4 %collective-permute-start.2 = (f32[16,1,32,128]{3,2,1,0:T(8,128)S(1)}, f32[16,1,32,128]{3,2,1,0:T(8,128)S(1)}, u32[]{:S(2)}, u32[]{:S(2)}) collective-permute-start(f32[16,1,32,128]{3,2,1,0:T(8,128)S(1)} %get-tuple-element.118), channel_id=1, source_target_pairs={{0,1},{1,2},{2,3},{3,4},{4,5},{5,6},{6,7},{8,9},{9,10},{10,11},{11... | collective-permute-start | bytes 786440 | tf_op jit(solution)/shard_map/ppermute | solution.py:19
  81.2 7.1 %collective-permute-start.3 = (f32[4,1,32,128]{3,2,1,0:T(8,128)S(1)}, f32[4,1,32,128]{3,2,1,0:T(8,128)S(1)}, u32[]{:S(2)}, u32[]{:S(2)}) collective-permute-start(f32[4,1,32,128]{3,2,1,0:T(8,128)S(1)} %get-tuple-element.139), channel_id=1, source_target_pairs={{1,0},{2,1},{3,2},{4,3},{5,4},{6,5},{7,6},{9,8},{10,9},{11,10},{12... | collective-permute-start | bytes 196616 | tf_op jit(solution)/shard_map/ppermute | solution.py:21
  82.5 6.6 %collective-permute-start.4 = (f32[4,1,32,128]{3,2,1,0:T(8,128)S(1)}, f32[4,1,32,128]{3,2,1,0:T(8,128)S(1)}, u32[]{:S(2)}, u32[]{:S(2)}) collective-permute-start(f32[4,1,32,128]{3,2,1,0:T(8,128)S(1)} %get-tuple-element.140), channel_id=1, source_target_pairs={{0,1},{1,2},{2,3},{3,4},{4,5},{5,6},{6,7},{8,9},{9,10},{10,11},{11... | collective-permute-start | bytes 196616 | tf_op jit(solution)/shard_map/ppermute | solution.py:19
  89.4 6.9 %collective-permute-start.5 = (f32[4,1,32,128]{3,2,1,0:T(8,128)S(1)}, f32[4,1,32,128]{3,2,1,0:T(8,128)S(1)}, u32[]{:S(2)}, u32[]{:S(2)}) collective-permute-start(f32[4,1,32,128]{3,2,1,0:T(8,128)S(1)} %get-tuple-element.133), channel_id=1, source_target_pairs={{1,0},{2,1},{3,2},{4,3},{5,4},{6,5},{7,6},{9,8},{10,9},{11,10},{12... | collective-permute-start | bytes 196616 | tf_op jit(solution)/shard_map/ppermute | solution.py:21
  90.7 6.3 %collective-permute-start.6 = (f32[4,1,32,128]{3,2,1,0:T(8,128)S(1)}, f32[4,1,32,128]{3,2,1,0:T(8,128)S(1)}, u32[]{:S(2)}, u32[]{:S(2)}) collective-permute-start(f32[4,1,32,128]{3,2,1,0:T(8,128)S(1)} %get-tuple-element.134), channel_id=1, source_target_pairs={{0,1},{1,2},{2,3},{3,4},{4,5},{5,6},{6,7},{8,9},{9,10},{10,11},{11... | collective-permute-start | bytes 196616 | tf_op jit(solution)/shard_map/ppermute | solution.py:19
  97.3 6.7 %collective-permute-start.7 = (f32[4,1,32,128]{3,2,1,0:T(8,128)S(1)}, f32[4,1,32,128]{3,2,1,0:T(8,128)S(1)}, u32[]{:S(2)}, u32[]{:S(2)}) collective-permute-start(f32[4,1,32,128]{3,2,1,0:T(8,128)S(1)} %get-tuple-element.127), channel_id=1, source_target_pairs={{1,0},{2,1},{3,2},{4,3},{5,4},{6,5},{7,6},{9,8},{10,9},{11,10},{12... | collective-permute-start | bytes 196616 | tf_op jit(solution)/shard_map/ppermute | solution.py:21
  98.6 6.2 %collective-permute-start.8 = (f32[4,1,32,128]{3,2,1,0:T(8,128)S(1)}, f32[4,1,32,128]{3,2,1,0:T(8,128)S(1)}, u32[]{:S(2)}, u32[]{:S(2)}) collective-permute-start(f32[4,1,32,128]{3,2,1,0:T(8,128)S(1)} %get-tuple-element.128), channel_id=1, source_target_pairs={{0,1},{1,2},{2,3},{3,4},{4,5},{5,6},{6,7},{8,9},{9,10},{10,11},{11... | collective-permute-start | bytes 196616 | tf_op jit(solution)/shard_map/ppermute | solution.py:19
  105.1 6.1 %collective-permute-start.10 = (f32[4,1,32,128]{3,2,1,0:T(8,128)S(1)}, f32[4,1,32,128]{3,2,1,0:T(8,128)S(1)}, u32[]{:S(2)}, u32[]{:S(2)}) collective-permute-start(f32[4,1,32,128]{3,2,1,0:T(8,128)S(1)} %get-tuple-element.126), channel_id=1, source_target_pairs={{0,1},{1,2},{2,3},{3,4},{4,5},{5,6},{6,7},{8,9},{9,10},{10,11},{11... | collective-permute-start | bytes 196616 | tf_op jit(solution)/shard_map/ppermute | solution.py:19
  109.8 5.0 %collective-permute-start.9 = (f32[4,1,32,128]{3,2,1,0:T(8,128)S(1)}, f32[4,1,32,128]{3,2,1,0:T(8,128)S(1)}, u32[]{:S(2)}, u32[]{:S(2)}) collective-permute-start(f32[4,1,32,128]{3,2,1,0:T(8,128)S(1)} %get-tuple-element.125), channel_id=1, source_target_pairs={{1,0},{2,1},{3,2},{4,3},{5,4},{6,5},{7,6},{9,8},{10,9},{11,10},{12... | collective-permute-start | bytes 196616 | tf_op jit(solution)/shard_map/ppermute | solution.py:21
  114.8 1.0 copy-start.3
where the time goes:
time: 200 us; the launch traced here: 199 us
  blocking collectives  151 us (76%)
  starting transfers between devices  30.8 us (15%)
  waiting for transfers between devices  5.94 us (3%)
  other arithmetic  4.62 us (2%)
  local copies, waits for them, and re-layouts  4.36 us (2%)
  between operations  2.59 us (1%)
    psum x4, blocking collectives, broadcast(): return lax.psum(jnp.where(mine, x, jnp.zeros_like(x)), axis)  70 us
    psum x1, blocking collectives, shards(): projection = lax.psum(local_proj, ('harm', 'slab')) / entries  40.9 us
    psum x1, blocking collectives, shards(): square = lax.psum(jnp.sum(residue * residue), ('harm', 'slab')) / entries  39.9 us
    ppermute x5, starting transfers between devices, padded_2(): lax.ppermute(tail, axis, [(i, (i + 1) % count) for i in range(ends)])  24.2 us
    ppermute x5, starting transfers between devices, padded_2(): lax.ppermute(head, axis, [((i + 1) % count, i) for i in range(ends)])  6.46 us
  transfers between devices with their start and end apart: 13, of which 4 were waited for; matrix products, arithmetic and copies ran while one was open for 1% of the time, Pallas kernels for 0%

commit v1 on v0

--- a/solution.py
+++ b/solution.py
@@ -115,7 +115,7 @@
         * cell_shape[3]
     )
     local_proj = jnp.sum(vectors * solution[None], axis=(1, 2, 3, 4))
-    projection = lax.psum(local_proj, ("harm", "slab")) / entries
+    projection = lax.psum(lax.psum(local_proj, "slab"), "harm") / entries
     residue = solution - jnp.sum(projection[:, None, None, None, None] * vectors, axis=0)
     square = lax.psum(jnp.sum(residue * residue), ("harm", "slab")) / entries
     norm_value = jnp.sqrt(square + epsilon)

time: 200 us -> 182 us (0.910)
  blocking collectives: 151 us -> 132 us
    psum x1 -> x2, blocking collectives: 40.9 us -> 24 us  [shards(): projection = lax.psum(lax.psum(local_proj, 'slab'), 'harm') / entries]
    psum x1, blocking collectives: 39.9 us -> 37.6 us  [shards(): square = lax.psum(jnp.sum(residue * residue), ('harm', 'slab')) / entries]
where the time goes in v1:
time: 182 us; the launch traced here: 180 us
  blocking collectives  132 us (73%)
  starting transfers between devices  30.8 us (17%)
  waiting for transfers between devices  5.94 us (3%)
  other arithmetic  4.62 us (3%)
  local copies, waits for them, and re-layouts  4.36 us (2%)
  between operations  2.59 us (1%)
    psum x4, blocking collectives, broadcast(): return lax.psum(jnp.where(mine, x, jnp.zeros_like(x)), axis)  70 us
    psum x1, blocking collectives, shards(): square = lax.psum(jnp.sum(residue * residue), ('harm', 'slab')) / entries  37.6 us
    ppermute x5, starting transfers between devices, padded_2(): lax.ppermute(tail, axis, [(i, (i + 1) % count) for i in range(ends)])  24.2 us
    psum x2, blocking collectives, shards(): projection = lax.psum(lax.psum(local_proj, 'slab'), 'harm') / entries  24 us
    ppermute x5, starting transfers between devices, padded_2(): lax.ppermute(head, axis, [((i + 1) % count, i) for i in range(ends)])  6.46 us
  transfers between devices with their start and end apart: 13, of which 4 were waited for; matrix products, arithmetic and copies ran while one was open for 1% of the time, Pallas kernels for 0%

profile of v1, /device:TPU:0, one launch (start us, length us, event | category | flops | bytes accessed | tf_op | source)
XLA Modules:
  0.0 180.1 jit_solution(5977175104541114848)
XLA Ops:
  0.6 0.0 copy-start.5
  0.7 0.6 copy-done.5
  1.3 1.1 fusion
  2.4 0.0 copy-start
  2.4 0.0 copy-start.4
  2.4 0.6 copy-done
  3.1 0.2 copy-done.4
  3.3 18.4 %psum.39 = bf16[3,2,32,128]{3,2,1,0:T(8,128)(2,1)S(1)} all-reduce(bf16[3,2,32,128]{3,2,1,0:T(8,128)(2,1)S(1)} %broadcast_select_fusion.1), channel_id=1, replica_groups=mesh['harm'=4,'slab'=8] {'harm'}, use_global_device_ids=true, to_apply=%region_4.5 | all-reduce | flops 24576 | bytes 98304 | tf_op jit(solution)/shard_map/psum | solution.py:30
  21.7 52.6 %while.16 = (s32[]{:T(128)}, f32[3,4,2,32,128]{4,3,2,1,0:T(8,128)S(1)}, f32[4,2,32,128]{3,2,1,0:T(8,128)S(1)}, bf16[3,2,32,128]{3,2,1,0:T(8,128)(2,1)S(1)}, s32[]{:T(128)}, /*index=5*/u32[]{:T(128)}, s32[]{:T(128)}) while((s32[]{:T(128)}, f32[3,4,2,32,128]{4,3,2,1,0:T(8,128)S(1)}, f32[4,2,32,128]{3,2,1,0:T(8,128)S(1)}, ...), condition=%wide.region_3.4_spmd.clone, body=%wide.region_1.3_spmd.clone.sunk | while | flops 368647 | bytes 2146473 | solution.py:99
  21.7 0.1 collective-permute-start
  21.8 17.2 %psum.45 = bf16[3,2,32,128]{3,2,1,0:T(8,128)(2,1)S(1)} all-reduce(bf16[3,2,32,128]{3,2,1,0:T(8,128)(2,1)S(1)} %broadcast_select_fusion.3), channel_id=1, replica_groups=mesh['harm'=4,'slab'=8] {'harm'}, use_global_device_ids=true, to_apply=%region_2.2 | all-reduce | flops 24576 | bytes 98304 | tf_op jit(solution)/shard_map/while/body/eval_jaxpr/psum | solution.py:30
  39.1 0.1 select_add_fusion.2
  39.2 0.0 collective-permute-done
  39.3 0.1 collective-permute-start
  39.4 17.3 %psum.45 = bf16[3,2,32,128]{3,2,1,0:T(8,128)(2,1)S(1)} all-reduce(bf16[3,2,32,128]{3,2,1,0:T(8,128)(2,1)S(1)} %broadcast_select_fusion.3), channel_id=1, replica_groups=mesh['harm'=4,'slab'=8] {'harm'}, use_global_device_ids=true, to_apply=%region_2.2 | all-reduce | flops 24576 | bytes 98304 | tf_op jit(solution)/shard_map/while/body/eval_jaxpr/psum | solution.py:30
  56.7 0.1 select_add_fusion.2
  56.8 0.1 collective-permute-start
  56.9 17.1 %psum.45 = bf16[3,2,32,128]{3,2,1,0:T(8,128)(2,1)S(1)} all-reduce(bf16[3,2,32,128]{3,2,1,0:T(8,128)(2,1)S(1)} %broadcast_select_fusion.3), channel_id=1, replica_groups=mesh['harm'=4,'slab'=8] {'harm'}, use_global_device_ids=true, to_apply=%region_2.2 | all-reduce | flops 24576 | bytes 98304 | tf_op jit(solution)/shard_map/while/body/eval_jaxpr/psum | solution.py:30
  74.1 0.1 select_add_fusion.2
  74.2 0.0 collective-permute-done
  74.3 0.0 copy-start.1
  74.3 0.1 multiply_add_fusion
  74.3 0.8 copy-done.1
  75.2 1.3 collective-permute-start.1
  76.5 3.0 %collective-permute-start.2 = (f32[16,1,32,128]{3,2,1,0:T(8,128)S(1)}, f32[16,1,32,128]{3,2,1,0:T(8,128)S(1)}, u32[]{:S(2)}, u32[]{:S(2)}) collective-permute-start(f32[16,1,32,128]{3,2,1,0:T(8,128)S(1)} %get-tuple-element.118), channel_id=1, source_target_pairs={{0,1},{1,2},{2,3},{3,4},{4,5},{5,6},{6,7},{8,9},{9,10},{10,11},{11... | collective-permute-start | bytes 786440 | tf_op jit(solution)/shard_map/ppermute | solution.py:19
  79.6 0.1 fusion.69
  79.7 0.1 fusion.70
  79.8 0.1 fusion.67
  80.8 0.1 fusion.68
  80.9 0.0 collective-permute-done.1
  80.9 0.2 broadcast_divide_fusion
  81.1 0.1 fusion.65
  81.2 1.3 collective-permute-start.3
  82.5 5.7 %collective-permute-start.4 = (f32[4,1,32,128]{3,2,1,0:T(8,128)S(1)}, f32[4,1,32,128]{3,2,1,0:T(8,128)S(1)}, u32[]{:S(2)}, u32[]{:S(2)}) collective-permute-start(f32[4,1,32,128]{3,2,1,0:T(8,128)S(1)} %get-tuple-element.140), channel_id=1, source_target_pairs={{0,1},{1,2},{2,3},{3,4},{4,5},{5,6},{6,7},{8,9},{9,10},{10,11},{11... | collective-permute-start | bytes 196616 | tf_op jit(solution)/shard_map/ppermute | solution.py:19
  88.2 0.1 fusion.66
  88.3 0.8 collective-permute-done.4
  89.1 0.1 multiply_add_fusion.3
  89.3 0.1 fusion.62
  89.4 1.3 collective-permute-start.5
  90.7 5.4 %collective-permute-start.6 = (f32[4,1,32,128]{3,2,1,0:T(8,128)S(1)}, f32[4,1,32,128]{3,2,1,0:T(8,128)S(1)}, u32[]{:S(2)}, u32[]{:S(2)}) collective-permute-start(f32[4,1,32,128]{3,2,1,0:T(8,128)S(1)} %get-tuple-element.134), channel_id=1, source_target_pairs={{0,1},{1,2},{2,3},{3,4},{4,5},{5,6},{6,7},{8,9},{9,10},{10,11},{11... | collective-permute-start | bytes 196616 | tf_op jit(solution)/shard_map/ppermute | solution.py:19
  96.1 0.1 fusion.63
  96.2 0.8 collective-permute-done.6
  97.0 0.1 multiply_add_fusion.2
  97.2 0.1 fusion.59
  97.3 1.3 collective-permute-start.7
  98.6 5.3 %collective-permute-start.8 = (f32[4,1,32,128]{3,2,1,0:T(8,128)S(1)}, f32[4,1,32,128]{3,2,1,0:T(8,128)S(1)}, u32[]{:S(2)}, u32[]{:S(2)}) collective-permute-start(f32[4,1,32,128]{3,2,1,0:T(8,128)S(1)} %get-tuple-element.128), channel_id=1, source_target_pairs={{0,1},{1,2},{2,3},{3,4},{4,5},{5,6},{6,7},{8,9},{9,10},{10,11},{11... | collective-permute-start | bytes 196616 | tf_op jit(solution)/shard_map/ppermute | solution.py:19
  103.9 0.1 fusion.60
  104.0 0.8 collective-permute-done.8
  104.8 0.1 multiply_add_fusion.1
  104.9 0.1 fusion.55
  105.1 4.7 %collective-permute-start.10 = (f32[4,1,32,128]{3,2,1,0:T(8,128)S(1)}, f32[4,1,32,128]{3,2,1,0:T(8,128)S(1)}, u32[]{:S(2)}, u32[]{:S(2)}) collective-permute-start(f32[4,1,32,128]{3,2,1,0:T(8,128)S(1)} %get-tuple-element.126), channel_id=1, source_target_pairs={{0,1},{1,2},{2,3},{3,4},{4,5},{5,6},{6,7},{8,9},{9,10},{10,11},{11... | collective-permute-start | bytes 196616 | tf_op jit(solution)/shard_map/ppermute | solution.py:19
  109.8 1.3 collective-permute-start.9
  111.1 0.1 fusion.56
  111.2 3.6 %collective-permute-done.9 = f32[4,1,32,128]{3,2,1,0:T(8,128)S(1)} collective-permute-done((f32[4,1,32,128]{3,2,1,0:T(8,128)S(1)}, f32[4,1,32,128]{3,2,1,0:T(8,128)S(1)}, u32[]{:S(2)}, u32[]{:S(2)}) %collective-permute-start.9) | collective-permute-done | bytes 65568 | tf_op jit(solution)/shard_map/ppermute | solution.py:21
  114.8 0.2 fusion.45
  114.9 0.8 copy-done.3
  115.8 0.1 fusion.1
  115.9 16.5 %psum.40 = f32[3]{0:T(128)S(1)} all-reduce(f32[3]{0:T(128)S(1)} %fusion.1), channel_id=1, replica_groups=mesh['harm'=4,'slab'=8] {'slab'}, use_global_device_ids=true, to_apply=%region_6.7 | all-reduce | flops 3 | bytes 24 | tf_op jit(solution)/shard_map/psum | solution.py:118
  132.4 7.5 %psum.41 = f32[3]{0:T(128)S(1)} all-reduce(f32[3]{0:T(128)S(1)} %psum.40), channel_id=1, replica_groups=mesh['harm'=4,'slab'=8] {'harm'}, use_global_device_ids=true, to_apply=%region_7.8 | all-reduce | flops 3 | bytes 24 | tf_op jit(solution)/shard_map/psum | solution.py:118
  139.9 0.1 fusion.2
  140.0 0.6 multiply_reduce_fusion
  140.6 37.6 %psum.42 = f32[]{:T(128)} all-reduce(f32[]{:T(128)} %get-tuple-element.107), channel_id=1, replica_groups=mesh['harm'=4,'slab'=8] {'harm','slab'}, use_global_device_ids=true, to_apply=%region_10.11 | all-reduce | flops 1 | bytes 8 | tf_op jit(solution)/shard_map/psum | solution.py:120
  178.9 0.6 pad_maximum_fusion.13
  179.5 0.7 divide_bitcast_fusion
  (28 shorter events, 0.2 us)
Async XLA Ops:
  0.6 0.7 copy-start.5
  2.4 0.7 copy-start
  2.4 0.8 copy-start.4
  3.3 18.4 %copy-start.2 = (f32[4,2,32,128]{3,2,1,0:T(8,128)S(1)}, f32[4,2,32,128]{3,2,1,0:T(8,128)}, u32[]{:S(2)}) copy-start(f32[4,2,32,128]{3,2,1,0:T(8,128)} %copy-done) | copy-start | bytes 393220
  21.7 17.5 %collective-permute-start = (f32[4,2,32,128]{3,2,1,0:T(8,128)S(1)}, f32[4,2,32,128]{3,2,1,0:T(8,128)S(1)}, u32[]{:S(2)}, u32[]{:S(2)}) collective-permute-start(f32[4,2,32,128]{3,2,1,0:T(8,128)S(1)} %copy.11), channel_id=1, source_target_pairs={{0,8},{8,16},{16,24},{24,0},{1,9},{9,17},{17,25},{25,1},{2,10},{10... | collective-permute-start | bytes 393224 | tf_op jit(solution)/shard_map/while/body/eval_jaxpr/ppermute | solution.py:36
  39.3 17.5 %collective-permute-start = (f32[4,2,32,128]{3,2,1,0:T(8,128)S(1)}, f32[4,2,32,128]{3,2,1,0:T(8,128)S(1)}, u32[]{:S(2)}, u32[]{:S(2)}) collective-permute-start(f32[4,2,32,128]{3,2,1,0:T(8,128)S(1)} %copy.11), channel_id=1, source_target_pairs={{0,8},{8,16},{16,24},{24,0},{1,9},{9,17},{17,25},{25,1},{2,10},{10... | collective-permute-start | bytes 393224 | tf_op jit(solution)/shard_map/while/body/eval_jaxpr/ppermute | solution.py:36
  56.8 17.4 %collective-permute-start = (f32[4,2,32,128]{3,2,1,0:T(8,128)S(1)}, f32[4,2,32,128]{3,2,1,0:T(8,128)S(1)}, u32[]{:S(2)}, u32[]{:S(2)}) collective-permute-start(f32[4,2,32,128]{3,2,1,0:T(8,128)S(1)} %copy.11), channel_id=1, source_target_pairs={{0,8},{8,16},{16,24},{24,0},{1,9},{9,17},{17,25},{25,1},{2,10},{10... | collective-permute-start | bytes 393224 | tf_op jit(solution)/shard_map/while/body/eval_jaxpr/ppermute | solution.py:36
  74.3 0.9 copy-start.1
  75.2 5.7 %collective-permute-start.1 = (f32[16,1,32,128]{3,2,1,0:T(8,128)S(1)}, f32[16,1,32,128]{3,2,1,0:T(8,128)S(1)}, u32[]{:S(2)}, u32[]{:S(2)}) collective-permute-start(f32[16,1,32,128]{3,2,1,0:T(8,128)S(1)} %get-tuple-element.117), channel_id=1, source_target_pairs={{1,0},{2,1},{3,2},{4,3},{5,4},{6,5},{7,6},{9,8},{10,9},{11,10},{12... | collective-permute-start | bytes 786440 | tf_op jit(solution)/shard_map/ppermute | solution.py:21
  76.5 4.4 %collective-permute-start.2 = (f32[16,1,32,128]{3,2,1,0:T(8,128)S(1)}, f32[16,1,32,128]{3,2,1,0:T(8,128)S(1)}, u32[]{:S(2)}, u32[]{:S(2)}) collective-permute-start(f32[16,1,32,128]{3,2,1,0:T(8,128)S(1)} %get-tuple-element.118), channel_id=1, source_target_pairs={{0,1},{1,2},{2,3},{3,4},{4,5},{5,6},{6,7},{8,9},{9,10},{10,11},{11... | collective-permute-start | bytes 786440 | tf_op jit(solution)/shard_map/ppermute | solution.py:19
  81.2 7.1 %collective-permute-start.3 = (f32[4,1,32,128]{3,2,1,0:T(8,128)S(1)}, f32[4,1,32,128]{3,2,1,0:T(8,128)S(1)}, u32[]{:S(2)}, u32[]{:S(2)}) collective-permute-start(f32[4,1,32,128]{3,2,1,0:T(8,128)S(1)} %get-tuple-element.139), channel_id=1, source_target_pairs={{1,0},{2,1},{3,2},{4,3},{5,4},{6,5},{7,6},{9,8},{10,9},{11,10},{12... | collective-permute-start | bytes 196616 | tf_op jit(solution)/shard_map/ppermute | solution.py:21
  82.5 6.6 %collective-permute-start.4 = (f32[4,1,32,128]{3,2,1,0:T(8,128)S(1)}, f32[4,1,32,128]{3,2,1,0:T(8,128)S(1)}, u32[]{:S(2)}, u32[]{:S(2)}) collective-permute-start(f32[4,1,32,128]{3,2,1,0:T(8,128)S(1)} %get-tuple-element.140), channel_id=1, source_target_pairs={{0,1},{1,2},{2,3},{3,4},{4,5},{5,6},{6,7},{8,9},{9,10},{10,11},{11... | collective-permute-start | bytes 196616 | tf_op jit(solution)/shard_map/ppermute | solution.py:19
  89.4 6.9 %collective-permute-start.5 = (f32[4,1,32,128]{3,2,1,0:T(8,128)S(1)}, f32[4,1,32,128]{3,2,1,0:T(8,128)S(1)}, u32[]{:S(2)}, u32[]{:S(2)}) collective-permute-start(f32[4,1,32,128]{3,2,1,0:T(8,128)S(1)} %get-tuple-element.133), channel_id=1, source_target_pairs={{1,0},{2,1},{3,2},{4,3},{5,4},{6,5},{7,6},{9,8},{10,9},{11,10},{12... | collective-permute-start | bytes 196616 | tf_op jit(solution)/shard_map/ppermute | solution.py:21
  90.7 6.3 %collective-permute-start.6 = (f32[4,1,32,128]{3,2,1,0:T(8,128)S(1)}, f32[4,1,32,128]{3,2,1,0:T(8,128)S(1)}, u32[]{:S(2)}, u32[]{:S(2)}) collective-permute-start(f32[4,1,32,128]{3,2,1,0:T(8,128)S(1)} %get-tuple-element.134), channel_id=1, source_target_pairs={{0,1},{1,2},{2,3},{3,4},{4,5},{5,6},{6,7},{8,9},{9,10},{10,11},{11... | collective-permute-start | bytes 196616 | tf_op jit(solution)/shard_map/ppermute | solution.py:19
  97.3 6.7 %collective-permute-start.7 = (f32[4,1,32,128]{3,2,1,0:T(8,128)S(1)}, f32[4,1,32,128]{3,2,1,0:T(8,128)S(1)}, u32[]{:S(2)}, u32[]{:S(2)}) collective-permute-start(f32[4,1,32,128]{3,2,1,0:T(8,128)S(1)} %get-tuple-element.127), channel_id=1, source_target_pairs={{1,0},{2,1},{3,2},{4,3},{5,4},{6,5},{7,6},{9,8},{10,9},{11,10},{12... | collective-permute-start | bytes 196616 | tf_op jit(solution)/shard_map/ppermute | solution.py:21
  98.6 6.2 %collective-permute-start.8 = (f32[4,1,32,128]{3,2,1,0:T(8,128)S(1)}, f32[4,1,32,128]{3,2,1,0:T(8,128)S(1)}, u32[]{:S(2)}, u32[]{:S(2)}) collective-permute-start(f32[4,1,32,128]{3,2,1,0:T(8,128)S(1)} %get-tuple-element.128), channel_id=1, source_target_pairs={{0,1},{1,2},{2,3},{3,4},{4,5},{5,6},{6,7},{8,9},{9,10},{10,11},{11... | collective-permute-start | bytes 196616 | tf_op jit(solution)/shard_map/ppermute | solution.py:19
  105.1 6.1 %collective-permute-start.10 = (f32[4,1,32,128]{3,2,1,0:T(8,128)S(1)}, f32[4,1,32,128]{3,2,1,0:T(8,128)S(1)}, u32[]{:S(2)}, u32[]{:S(2)}) collective-permute-start(f32[4,1,32,128]{3,2,1,0:T(8,128)S(1)} %get-tuple-element.126), channel_id=1, source_target_pairs={{0,1},{1,2},{2,3},{3,4},{4,5},{5,6},{6,7},{8,9},{9,10},{10,11},{11... | collective-permute-start | bytes 196616 | tf_op jit(solution)/shard_map/ppermute | solution.py:19
  109.8 5.0 %collective-permute-start.9 = (f32[4,1,32,128]{3,2,1,0:T(8,128)S(1)}, f32[4,1,32,128]{3,2,1,0:T(8,128)S(1)}, u32[]{:S(2)}, u32[]{:S(2)}) collective-permute-start(f32[4,1,32,128]{3,2,1,0:T(8,128)S(1)} %get-tuple-element.125), channel_id=1, source_target_pairs={{1,0},{2,1},{3,2},{4,3},{5,4},{6,5},{7,6},{9,8},{10,9},{11,10},{12... | collective-permute-start | bytes 196616 | tf_op jit(solution)/shard_map/ppermute | solution.py:21
  114.8 1.0 copy-start.3
